TPU v7x, 128 devices: a whole 4x4x4 slice. The times are simulated.
128 devices in a mesh: occ: 8 (over y, core), vir: 16 (over x, z).
Axes of the slice: x: 4, y: 4, z: 4, core: 2. Of those that a mesh axis runs over, the one named last changes fastest.
Arguments:
- amplitudes: bfloat16 [4096, 49152], P('occ', 'vir'), may hold values from -6 to 6
- integral_tiles: bfloat16 [16, 256, 128, 128], P('vir', 'occ'), may hold values from -0.0625 to 0.0625
- tile_cd: int32 [16, 256], replicated, may hold values from 0 to 23, as said below
- tile_ab: int32 [16, 256], replicated, may hold values from 0 to 63, as said below
- slot_tile: int32 [64], replicated, may hold values from 0 to 63, as said below
- residual_in: float32 [4096, 8192], P('occ', 'vir'), may hold values from -6 to 6
- occ_level: float32 [4096], P('occ'), may hold values from -3 to -1
- vir_level: float32 [8192], P('vir'), may hold values from 0.5 to 3
Outputs:
- update: float32 [4096, 8192], P('occ', 'vir')
Inputs may be any that keep to these rules, and one draw needn't show every extreme that they name: `tile_cd`: within a group no pair of contracted tile and slab tile repeats. `tile_ab`: for every group and every index w of vir, the group's tiles name slab tiles held in exactly 2 of the slots w * 4 to (w + 1) * 4 - 1. `slot_tile`: A permutation of the slab tiles.
All inputs are finite; a program needn't handle non-finite values.
Results may differ from a plain program's by a relative error of at most 0.0003.
Values may be sent and summed in bfloat16 or wider, within the bound.
A program may use at most 128 MiB of HBM per device.

v0:
```python
import jax
import jax.numpy as jnp
from jax import lax
from jax.sharding import PartitionSpec as P

CAP = 2


def slot_numbers(ab_tiles, slot_tile):
    match = ab_tiles[..., None] == slot_tile
    places = lax.broadcasted_iota(jnp.int32, match.shape, match.ndim - 1)
    return jnp.sum(jnp.where(match, places, 0), axis=-1)


def shards(
    amplitudes, integral_tiles, tile_cd, tile_ab, slot_tile, residual_in, occ_level, vir_level
):
    groups = lax.axis_size("vir")
    mine = lax.axis_index("vir")
    rows = amplitudes.shape[0]
    tile = integral_tiles.shape[-1]
    kind_count = amplitudes.shape[1] // tile
    total_slots = slot_tile.shape[0]
    per_owner = total_slots // groups
    slots_all = slot_numbers(tile_ab, slot_tile)
    every_slot = jnp.arange(total_slots, dtype=jnp.int32)
    reached = jnp.any(slots_all[..., None] == every_slot, axis=1).astype(jnp.int32)
    reached = reached.reshape(groups, groups, per_owner)
    rank = jnp.cumsum(reached, axis=-1) - 1
    picks = jnp.arange(CAP, dtype=jnp.int32)
    hit = (reached[..., None] == 1) & (rank[..., None] == picks)
    within = lax.broadcasted_iota(jnp.int32, hit.shape, 2)
    chosen = jnp.sum(jnp.where(hit, within, 0), axis=2)
    my_kinds = lax.dynamic_index_in_dim(tile_cd, mine, 0, keepdims=False)
    my_slots = lax.dynamic_index_in_dim(slots_all, mine, 0, keepdims=False)
    my_chosen = lax.dynamic_index_in_dim(chosen, mine, 0, keepdims=False)
    owner_of = my_slots // per_owner
    inside = my_slots % per_owner
    candidates = jnp.take(my_chosen, owner_of, axis=0)
    match = candidates == inside[:, None]
    cap_iota = lax.broadcasted_iota(jnp.int32, match.shape, 1)
    column_of = owner_of * CAP + jnp.sum(jnp.where(match, cap_iota, 0), axis=1)
    empty = jnp.zeros((groups * CAP, kind_count, tile, tile), jnp.bfloat16)
    weight = empty.at[column_of, my_kinds].set(
        lax.all_gather(integral_tiles, "occ", axis=1, tiled=True)[0]
    )
    left = amplitudes.reshape(rows, kind_count, tile)
    partial_value = jnp.einsum("rkt,ckts->rcs", left, weight, preferred_element_type=jnp.float32)
    owner_base = jnp.arange(groups, dtype=jnp.int32)[:, None] * per_owner
    places = (owner_base + my_chosen).reshape(-1)
    placing = (places[:, None] == every_slot[None, :]).astype(jnp.float32)
    spread = jnp.einsum("rcs,cq->rqs", partial_value, placing, precision=lax.Precision.HIGHEST)
    summed = lax.psum_scatter(spread, "vir", scatter_dimension=1, tiled=True)
    by_slot = summed.reshape(rows, per_owner * tile)
    return (residual_in + by_slot) / (occ_level[:, None] - vir_level[None, :])


def solution(mesh):
    in_specs = (
        P("occ", "vir"),
        P("vir", "occ", None, None),
        P(),
        P(),
        P(),
        P("occ", "vir"),
        P("occ"),
        P("vir"),
    )
    out_specs = P("occ", "vir")
    return jax.shard_map(shards, mesh=mesh, in_specs=in_specs, out_specs=out_specs, check_vma=False)
```

profile of v0, /device:TPU:1, one launch (start us, length us, event | category | flops | bytes accessed | tf_op | source)
XLA Modules:
  0.0 295.3 jit_solution(15879185883777184707)
XLA Ops:
  6.5 0.7 all-gather.2.cloned.1.call-update
  7.3 1.1 select_reduce_fusion
  8.4 0.4 fusion.2
  8.8 0.1 copy.35
  9.0 0.1 copy.36
  9.2 0.1 copy.38
  9.3 0.1 copy.39
  9.4 0.1 squeeze.18
  9.5 0.1 add.113
  9.7 0.7 gather_fusion
  10.4 0.2 select_reduce_fusion.1
  10.6 0.7 or_select_fusion
  11.4 51.0 %all-gather.2.cloned.1.call-done = bf16[1,256,128,128]{3,2,0,1:T(8,128)(2,1)} async-done(((bf16[1,32,128,128]{3,2,0,1:T(8,128)(2,1)}), bf16[1,256,128,128]{3,2,0,1:T(8,128)(2,1)}) %all-gather.2.cloned.1.call-update) | async-done | bytes 8388624 | tf_op jit(solution)/shard_map/all_gather | solution.py:45
  62.4 8.8 %broadcast_in_dim.40 = bf16[32,24,128,128]{3,2,1,0:T(8,128)(2,1)} broadcast(bf16[]{:T(256)} %constant.68.clone.1), dimensions={} | broadcast | bytes 25165826 | tf_op jit(solution)/shard_map/broadcast_in_dim | solution.py:43
  71.2 39.9 %scatter_fusion = bf16[32,24,128,128]{3,2,1,0:T(8,128)(2,1)} fusion(bf16[32,24,128,128]{3,2,1,0:T(8,128)(2,1)} %broadcast_in_dim.40, s32[256]{0:T(256)S(1)} %bitcast.45, bf16[256,128,128]{2,1,0:T(8,128)(2,1)} %bitcast.46), kind=kCustom, calls=%fused_computation.1 | custom fusion | bytes 25167872 | tf_op jit(solution)/shard_map/scatter | solution.py:44
  111.2 20.1 %convolution_bitcast_fusion.1 = f32[512,32,128]{0,2,1:T(8,128)} fusion(bf16[32,24,128,128]{3,2,1,0:T(8,128)(2,1)} %scatter_fusion, bf16[512,3072]{1,0:T(8,128)(2,1)S(1)} %copy-done), kind=kOutput, calls=%fused_computation.3 | convolution fusion | flops 12884901888 | bytes 36700160 | tf_op jit(solution)/shard_map/rkt,ckts->rcs/dot_general | solution.py:48
  131.2 10.3 %copy.43 = f32[512,32,128]{2,1,0:T(8,128)} copy(f32[512,32,128]{0,2,1:T(8,128)} %convolution_bitcast_fusion.1) | data formatting | bytes 16777216 | tf_op jit(solution)/shard_map/rkt,ckts->rcs/dot_general | solution.py:48
  141.5 9.4 %convolution_bitcast_fusion = f32[512,64,128]{2,1,0:T(8,128)S(1)} fusion(f32[512,32,128]{2,1,0:T(8,128)} %copy.43, s32[32]{0:T(128)S(1)} %add.115), kind=kOutput, calls=%fused_computation.2 | convolution fusion | flops 1610614784 | bytes 25165952 | tf_op jit(solution)/shard_map/rcs,cq->rqs/dot_general | solution.py:52
  150.9 19.5 %copy.44 = f32[512,64,128]{2,0,1:T(8,128)} copy(f32[512,64,128]{2,1,0:T(8,128)S(1)} %convolution_bitcast_fusion) | data formatting | bytes 33554432 | tf_op jit(solution)/shard_map/rcs,cq->rqs/transpose | solution.py:52
  170.5 2.7 copy.46
  173.1 107.4 %reduce-scatter.2.cloned.1.call-done = f32[512,4,128]{2,0,1:T(8,128)} async-done(((f32[512,64,128]{2,0,1:T(8,128)}), f32[512,4,128]{2,0,1:T(8,128)}) %reduce-scatter.2.cloned.1.call-update) | async-done | bytes 1048592 | tf_op jit(solution)/shard_map/reduce_scatter | solution.py:53
  280.5 2.5 copy.45
  283.1 2.8 fusion.1
  285.9 2.5 copy.47
  (25 shorter events, 0.4 us)
Async XLA Ops:
  6.5 104.6 %copy-start = (bf16[512,3072]{1,0:T(8,128)(2,1)S(1)}, bf16[512,3072]{1,0:T(8,128)(2,1)}, u32[]{:S(2)}) copy-start(bf16[512,3072]{1,0:T(8,128)(2,1)} %param.8) | copy-start | bytes 9437188
  6.5 55.8 %all-gather.2.cloned.1.call-start = ((), (), s32[]{:S(2)}) async-start(), calls=%async_computation.1 | async-start | bytes 9437184 | tf_op jit(solution)/shard_map/all_gather | solution.py:45
  7.3 273.3 %reduce-scatter.2.cloned.1.call-start = ((), (), s32[]{:S(2)}) async-start(), calls=%async_computation.2 | async-start | bytes 17825792 | tf_op jit(solution)/shard_map/reduce_scatter | solution.py:53
  170.4 112.7 %copy-start.2 = (f32[512]{0:T(512)S(1)}, f32[512]{0:T(512)}, u32[]{:S(2)}) copy-start(f32[512]{0:T(512)} %param.15) | copy-start | bytes 6148
  170.4 112.7 %copy-start.3 = (f32[512]{0:T(512)S(1)}, f32[512]{0:T(512)}, u32[]{:S(2)}) copy-start(f32[512]{0:T(512)} %param.14) | copy-start | bytes 6148
  170.4 118.0 %copy-start.1 = (bf16[512,3072]{1,0:T(8,128)(2,1)S(1)}, bf16[512,3072]{1,0:T(8,128)(2,1)}, u32[]{:S(2)}) copy-start(bf16[512,3072]{1,0:T(8,128)(2,1)} %param.8) | copy-start | bytes 9437188
Sparse Core Ops, SparseCore 0:
  9.0 53.2 all-gather.1
  170.6 109.9 reduce-scatter.1
where the time goes:
time: 296 us; the launch traced here: 295 us
  waiting for transfers between devices  159 us (54%)
  local copies, waits for them, and re-layouts  87.7 us (30%)
  matrix products  29.5 us (10%)
  between operations  13.5 us (5%)
  other arithmetic  5.33 us (2%)
    reduce_scatter x1, waiting for transfers between devices, shards(): summed = lax.psum_scatter(spread, 'vir', scatter_dimension=1, tiled=True)  107 us
    all_gather x1, waiting for transfers between devices, shards(): lax.all_gather(integral_tiles, 'occ', axis=1, tiled=True)[0]  51 us
    scatter x1, local copies, waits for them, and re-layouts, shards(): empty.at[column_of, my_kinds]  39.9 us
    dot_general x1, matrix products, shards(): jnp.einsum('rkt,ckts->rcs', left, weight, preferred_element_type=jnp.floa...  20.1 us
    transpose x1, local copies, waits for them, and re-layouts, shards(): jnp.einsum('rcs,cq->rqs', partial_value, placing, precision=lax.Precision...  19.5 us
    dot_general x1, local copies, waits for them, and re-layouts, shards(): jnp.einsum('rkt,ckts->rcs', left, weight, preferred_element_type=jnp.floa...  10.3 us
    dot_general x1, matrix products, shards(): jnp.einsum('rcs,cq->rqs', partial_value, placing, precision=lax.Precision...  9.42 us
    broadcast_in_dim x1, local copies, waits for them, and re-layouts, shards(): empty = jnp.zeros((groups * CAP, kind_count, tile, tile), jnp.bfloat16)  8.84 us
  transfers between devices with their start and end apart: 2, of which 2 were waited for; matrix products, arithmetic and copies ran while one was open for 2% of the time, Pallas kernels for 0%

commit v1 on v0

--- a/solution.py
+++ b/solution.py
@@ -42,7 +42,9 @@
     column_of = owner_of * CAP + jnp.sum(jnp.where(match, cap_iota, 0), axis=1)
     empty = jnp.zeros((groups * CAP, kind_count, tile, tile), jnp.bfloat16)
     weight = empty.at[column_of, my_kinds].set(
-        lax.all_gather(integral_tiles, "occ", axis=1, tiled=True)[0]
+        jnp.concatenate(
+            lax.all_to_all(jnp.stack([integral_tiles] * lax.axis_size("occ")), "occ", 0, 0), axis=1
+        )[0]
     )
     left = amplitudes.reshape(rows, kind_count, tile)
     partial_value = jnp.einsum("rkt,ckts->rcs", left, weight, preferred_element_type=jnp.float32)

time: 296 us -> 349 us (1.18)
  waiting for transfers between devices: 159 us -> 199 us
  local copies, waits for them, and re-layouts: 87.7 us -> 94.5 us
  starting transfers between devices: 0.04 us -> 6.43 us
    all_to_all x0 -> x1, waiting for transfers between devices: none -> 90.6 us  [shards(): lax.all_to_all(jnp.stack([integral_tiles] * lax.axis_size('occ')), 'occ',...]
    all_gather x1 -> x0, waiting for transfers between devices: 51 us -> none  [shards(): lax.all_gather(integral_tiles, 'occ', axis=1, tiled=True)[0]]
    another operation x0 -> x1, local copies, waits for them, and re-layouts: none -> 6.73 us  [shards(): jnp.stack([integral_tiles] * lax.axis_size('occ'))]
    all_to_all x0 -> x1, starting transfers between devices: none -> 6.43 us  [shards(): lax.all_to_all(jnp.stack([integral_tiles] * lax.axis_size('occ')), 'occ',...]
where the time goes in v1:
time: 349 us; the launch traced here: 348 us
  waiting for transfers between devices  199 us (57%)
  local copies, waits for them, and re-layouts  94.5 us (27%)
  matrix products  29.5 us (8%)
  between operations  13.5 us (4%)
  starting transfers between devices  6.43 us (2%)
  other arithmetic  4.44 us (1%)
    reduce_scatter x1, waiting for transfers between devices, shards(): summed = lax.psum_scatter(spread, 'vir', scatter_dimension=1, tiled=True)  109 us
    all_to_all x1, waiting for transfers between devices, shards(): lax.all_to_all(jnp.stack([integral_tiles] * lax.axis_size('occ')), 'occ',...  90.6 us
    scatter x1, local copies, waits for them, and re-layouts, shards(): empty.at[column_of, my_kinds]  39.9 us
    dot_general x1, matrix products, shards(): jnp.einsum('rkt,ckts->rcs', left, weight, preferred_element_type=jnp.floa...  20.1 us
    transpose x1, local copies, waits for them, and re-layouts, shards(): jnp.einsum('rcs,cq->rqs', partial_value, placing, precision=lax.Precision...  19.5 us
    dot_general x1, local copies, waits for them, and re-layouts, shards(): jnp.einsum('rkt,ckts->rcs', left, weight, preferred_element_type=jnp.floa...  10.3 us
    dot_general x1, matrix products, shards(): jnp.einsum('rcs,cq->rqs', partial_value, placing, precision=lax.Precision...  9.42 us
    broadcast_in_dim x1, local copies, waits for them, and re-layouts, shards(): empty = jnp.zeros((groups * CAP, kind_count, tile, tile), jnp.bfloat16)  8.84 us
  transfers between devices with their start and end apart: 2, of which 2 were waited for; matrix products, arithmetic and copies ran while one was open for 2% of the time, Pallas kernels for 0%

profile of v1, /device:TPU:1, one launch (start us, length us, event | category | flops | bytes accessed | tf_op | source)
XLA Modules:
  0.0 347.8 jit_solution(7738681374906345059)
XLA Ops:
  6.5 6.7 %stack.2 = bf16[8,1,32,128,128]{4,3,2,1,0:T(8,128)(2,1)} broadcast(bf16[32,128,128]{2,1,0:T(8,128)(2,1)} %bitcast.46), dimensions={2,3,4} | broadcast | bytes 9437184 | tf_op jit(solution)/shard_map/stack | solution.py:46
  13.3 6.4 %all-to-all-start = ((bf16[8,1,32,128,128]{4,3,2,1,0:T(8,128)(2,1)}), bf16[8,1,32,128,128]{4,3,2,1,0:T(8,128)(2,1)}, u32[]{:S(2)}, u32[]{:S(2)}) async-start(bf16[8,1,32,128,128]{4,3,2,1,0:T(8,128)(2,1)} %stack.2), calls=%async_computation | async-start | bytes 16777216 | tf_op jit(solution)/shard_map/all_to_all | solution.py:46
  19.7 0.2 select_reduce_fusion
  19.9 0.4 fusion.2
  20.3 0.1 copy.34
  20.6 0.1 copy.35
  20.7 0.1 copy.37
  20.9 0.1 squeeze.15
  21.0 0.1 add.113
  21.2 0.7 gather_fusion
  21.9 0.2 select_reduce_fusion.1
  22.2 0.7 or_select_fusion
  22.9 90.6 %all-to-all-done = bf16[8,1,32,128,128]{4,3,2,1,0:T(8,128)(2,1)} async-done(((bf16[8,1,32,128,128]{4,3,2,1,0:T(8,128)(2,1)}), bf16[8,1,32,128,128]{4,3,2,1,0:T(8,128)(2,1)}, u32[]{:S(2)}, u32[]{:S(2)}) %all-to-all-start) | async-done | bytes 8388640 | tf_op jit(solution)/shard_map/all_to_all | solution.py:46
  113.5 8.8 %broadcast_in_dim.40 = bf16[32,24,128,128]{3,2,1,0:T(8,128)(2,1)} broadcast(bf16[]{:T(256)} %constant.68.clone.1), dimensions={} | broadcast | bytes 25165826 | tf_op jit(solution)/shard_map/broadcast_in_dim | solution.py:43
  122.3 39.9 %scatter_fusion = bf16[32,24,128,128]{3,2,1,0:T(8,128)(2,1)} fusion(bf16[32,24,128,128]{3,2,1,0:T(8,128)(2,1)} %broadcast_in_dim.40, s32[256]{0:T(256)S(1)} %bitcast.45, bf16[256,128,128]{2,1,0:T(8,128)(2,1)} %bitcast.10), kind=kCustom, calls=%fused_computation.1 | custom fusion | bytes 25167872 | tf_op jit(solution)/shard_map/scatter | solution.py:44
  162.2 20.1 %convolution_bitcast_fusion.1 = f32[512,32,128]{0,2,1:T(8,128)} fusion(bf16[32,24,128,128]{3,2,1,0:T(8,128)(2,1)} %scatter_fusion, bf16[512,3072]{1,0:T(8,128)(2,1)S(1)} %copy-done), kind=kOutput, calls=%fused_computation.3 | convolution fusion | flops 12884901888 | bytes 36700160 | tf_op jit(solution)/shard_map/rkt,ckts->rcs/dot_general | solution.py:50
  182.3 10.3 %copy.41 = f32[512,32,128]{2,1,0:T(8,128)} copy(f32[512,32,128]{0,2,1:T(8,128)} %convolution_bitcast_fusion.1) | data formatting | bytes 16777216 | tf_op jit(solution)/shard_map/rkt,ckts->rcs/dot_general | solution.py:50
  192.6 9.4 %convolution_bitcast_fusion = f32[512,64,128]{2,1,0:T(8,128)S(1)} fusion(f32[512,32,128]{2,1,0:T(8,128)} %copy.41, s32[32]{0:T(128)S(1)} %add.115), kind=kOutput, calls=%fused_computation.2 | convolution fusion | flops 1610614784 | bytes 25165952 | tf_op jit(solution)/shard_map/rcs,cq->rqs/dot_general | solution.py:54
  202.0 19.5 %copy.42 = f32[512,64,128]{2,0,1:T(8,128)} copy(f32[512,64,128]{2,1,0:T(8,128)S(1)} %convolution_bitcast_fusion) | data formatting | bytes 33554432 | tf_op jit(solution)/shard_map/rcs,cq->rqs/transpose | solution.py:54
  221.6 2.7 copy.44
  224.3 108.8 %reduce-scatter.2.cloned.1.call-done = f32[512,4,128]{2,0,1:T(8,128)} async-done(((f32[512,64,128]{2,0,1:T(8,128)}), f32[512,4,128]{2,0,1:T(8,128)}) %reduce-scatter.2.cloned.1.call-update) | async-done | bytes 1048592 | tf_op jit(solution)/shard_map/reduce_scatter | solution.py:55
  333.1 2.5 copy.43
  335.7 2.8 fusion.1
  338.4 2.5 copy.45
  (29 shorter events, 0.5 us)
Async XLA Ops:
  6.5 155.7 %copy-start = (bf16[512,3072]{1,0:T(8,128)(2,1)S(1)}, bf16[512,3072]{1,0:T(8,128)(2,1)}, u32[]{:S(2)}) copy-start(bf16[512,3072]{1,0:T(8,128)(2,1)} %param.8) | copy-start | bytes 9437188
  13.3 6.4 %copy-start.2 = (s32[16,256]{1,0:T(8,128)S(1)}, s32[16,256]{1,0:T(8,128)}, u32[]{:S(2)}) copy-start(s32[16,256]{1,0:T(8,128)} %param.11) | copy-start | bytes 49156
  13.3 6.4 %copy-start.5 = (s32[64]{0:T(128)S(1)}, s32[64]{0:T(128)}, u32[]{:S(2)}) copy-start(s32[64]{0:T(128)} %param.12) | copy-start | bytes 772
  13.3 100.2 %all-to-all-start = ((bf16[8,1,32,128,128]{4,3,2,1,0:T(8,128)(2,1)}), bf16[8,1,32,128,128]{4,3,2,1,0:T(8,128)(2,1)}, u32[]{:S(2)}, u32[]{:S(2)}) async-start(bf16[8,1,32,128,128]{4,3,2,1,0:T(8,128)(2,1)} %stack.2), calls=%async_computation | async-start | bytes 16777216 | tf_op jit(solution)/shard_map/all_to_all | solution.py:46
  19.7 313.4 %reduce-scatter.2.cloned.1.call-start = ((), (), s32[]{:S(2)}) async-start(), calls=%async_computation.2 | async-start | bytes 17825792 | tf_op jit(solution)/shard_map/reduce_scatter | solution.py:55
  221.6 114.1 %copy-start.3 = (f32[512]{0:T(512)S(1)}, f32[512]{0:T(512)}, u32[]{:S(2)}) copy-start(f32[512]{0:T(512)} %param.15) | copy-start | bytes 6148
  221.6 114.1 %copy-start.4 = (f32[512]{0:T(512)S(1)}, f32[512]{0:T(512)}, u32[]{:S(2)}) copy-start(f32[512]{0:T(512)} %param.14) | copy-start | bytes 6148
  221.6 119.4 %copy-start.1 = (bf16[512,3072]{1,0:T(8,128)(2,1)S(1)}, bf16[512,3072]{1,0:T(8,128)(2,1)}, u32[]{:S(2)}) copy-start(bf16[512,3072]{1,0:T(8,128)(2,1)} %param.8) | copy-start | bytes 9437188
Sparse Core Ops, SparseCore 0:
  221.7 111.3 reduce-scatter.1
